TPU v7x, 256 devices: a whole 4x4x8 slice. The times are simulated.
256 devices in a mesh: gx: 8 (over z), gy: 16 (over y, x), sa: 2 (over core).
Axes of the slice: x: 4, y: 4, z: 8, core: 2. Of those that a mesh axis runs over, the one named last changes fastest.
Arguments:
- field: float32 [33, 32, 672, 256], P(None, 'gx', 'gy', 'sa'), as said below
- start: float32 [33, 16], replicated, may hold values from -1 to 1
Outputs:
- basis: float32 [33, 16], replicated
- gram_two: float32 [672, 672], P('gy', ('gx', 'sa'))
Inputs may be any that keep to these rules, and one draw needn't show every extreme that they name: `field`: every entry is finite; species differ in scale.
All inputs are finite; a program needn't handle non-finite values.
Results may differ from a plain program's by a relative error of at most 0.0003.
Values sent between devices are 32-bit elements; how exact they have to be, the bound alone decides.
A program may use at most 128 MiB of HBM per device.

v0:
```python
import jax
import jax.numpy as jnp
from jax import lax
from jax.sharding import PartitionSpec as P

ITERS = 4
HIGH = lax.Precision.HIGHEST


def orth(block):
    inner = jnp.dot(block.T, block, precision=HIGH, preferred_element_type=jnp.float32)
    lower = jnp.linalg.cholesky(inner)
    return jax.scipy.linalg.solve_triangular(lower, block.T, lower=True).T


def leading(gram, start, rounds):
    basis = orth(orth(start))
    for step in range(rounds):
        basis = orth(orth(jnp.dot(gram, basis, precision=HIGH, preferred_element_type=jnp.float32)))
    return basis


def project(basis, data):
    return jnp.einsum("sr,sxyz->rxyz", basis, data, precision=HIGH)


def line_gram(left, right):
    return jnp.einsum("rxiz,rxjz->ij", left, right, precision=HIGH)


def on_device(field, start):
    species, cells_x, cells_y, cells_z = field.shape
    ranks = start.shape[1]
    total_x = cells_x * lax.axis_size("gx")
    total_y = cells_y * lax.axis_size("gy")
    total_z = cells_z * lax.axis_size("sa")
    flat = field.reshape(species, -1)
    partial_gram = jnp.dot(flat, flat.T, precision=HIGH, preferred_element_type=jnp.float32)
    species_gram = lax.psum(partial_gram, ("gx", "gy", "sa")) / (total_x * total_y * total_z)
    basis = leading(species_gram, start, ITERS)
    core = project(basis, field)
    part_block = line_gram(core, lax.all_gather(core, "gy", axis=2, tiled=True))
    block = lax.psum_scatter(part_block, ("gx", "sa"), scatter_dimension=1, tiled=True) / (
        ranks * total_x * total_z
    )
    return (basis, block)


def solution(mesh):
    in_specs = (P(None, "gx", "gy", "sa"), P())
    out_specs = (P(), P("gy", ("gx", "sa")))
    return jax.shard_map(
        on_device, mesh=mesh, in_specs=in_specs, out_specs=out_specs, check_vma=False
    )
```

profile of v0, /device:TPU:1, one launch (start us, length us, event | category | flops | bytes accessed | tf_op | source)
XLA Modules:
  0.0 422.5 jit_solution(17980562996375337005)
XLA Ops:
  7.2 0.6 copy-done
  8.1 1.5 cholesky.164
  9.6 0.6 compare_reduce_fusion.9
  10.2 0.6 fusion.27
  10.9 1.2 custom-call.14
  12.1 0.2 fusion.69
  12.5 1.5 cholesky.175
  14.0 0.6 compare_reduce_fusion.8
  14.7 0.6 fusion.28
  15.3 1.2 custom-call.15
  16.6 0.2 fusion.66
  16.8 6.2 %fusion.12 = f32[33,33]{1,0:T(8,128)S(1)} fusion(f32[33,4,42,128]{3,1,2,0:T(4,128)} %param.5), kind=kOutput, calls=%fused_computation.8 | convolution fusion | flops 281014272 | bytes 2842884 | tf_op jit(solution)/shard_map/dot_general | solution.py:38
  22.9 81.5 %psum.7 = f32[33,33]{1,0:T(8,128)S(1)} all-reduce(f32[33,33]{1,0:T(8,128)S(1)} %fusion.12), channel_id=1, replica_groups=mesh['gx'=8,'gy'=16,'sa'=2] {'gx','gy','sa'}, use_global_device_ids=true, to_apply=%region_0.0 | all-reduce | flops 1089 | bytes 8712 | tf_op jit(solution)/shard_map/psum | solution.py:39
  104.6 0.1 fusion.97
  104.8 1.5 cholesky.186
  106.3 0.6 compare_reduce_fusion.7
  107.0 0.6 fusion.29
  107.6 1.2 custom-call.16
  108.9 0.2 fusion.62
  109.3 1.5 cholesky.197
  110.8 0.6 compare_reduce_fusion.6
  111.4 0.6 fusion.30
  112.1 1.2 custom-call.17
  113.3 0.2 fusion.59
  113.5 0.2 fusion.19
  113.9 1.5 cholesky.208
  115.4 0.6 compare_reduce_fusion.5
  116.0 0.6 fusion.31
  116.7 1.2 custom-call.18
  117.9 0.2 fusion.55
  118.4 1.5 cholesky.219
  119.9 0.6 compare_reduce_fusion.4
  120.5 0.6 fusion.32
  121.2 1.2 custom-call.19
  122.4 0.2 fusion.52
  122.6 0.2 fusion.17
  123.0 1.5 cholesky.230
  124.5 0.6 compare_reduce_fusion.3
  125.1 0.6 fusion.33
  125.8 1.2 custom-call.20
  127.0 0.2 fusion.48
  127.4 1.5 cholesky.241
  128.9 0.6 compare_reduce_fusion.2
  129.6 0.6 fusion.34
  130.2 1.2 custom-call.21
  131.5 0.2 fusion.45
  131.7 0.2 fusion.15
  132.0 1.5 cholesky.252
  133.5 0.6 compare_reduce_fusion.1
  134.2 0.6 fusion.35
  134.9 1.2 custom-call.22
  136.1 0.2 fusion.41
  136.5 1.5 cholesky.263
  138.0 0.6 compare_reduce_fusion
  138.7 0.6 fusion.36
  139.3 1.2 custom-call.23
  140.5 0.2 fusion.38
  140.8 3.4 fusion.2
  144.2 0.2 all-reduce.3.cloned.1.call-start
  144.4 138.0 %all-gather.2.cloned.1.call-done = f32[16,4,672,128]{3,0,2,1:T(8,128)} async-done(((f32[16,4,42,128]{3,0,2,1:T(8,128)}), f32[16,4,672,128]{3,0,2,1:T(8,128)}) %all-gather.2.cloned.1.call-update) | async-done | bytes 22020112 | tf_op jit(solution)/shard_map/all_gather | solution.py:42
  282.4 29.2 %fusion.7 = f32[42,672]{1,0:T(8,128)} fusion(f32[16,4,672,128]{3,0,2,1:T(8,128)} %all-gather.2.cloned.1.call-done, f32[16,4,42,128]{3,0,2,1:T(8,128)} %fusion.2), kind=kOutput, calls=%fused_computation.7 | convolution fusion | flops 2774532096 | bytes 23509248 | tf_op jit(solution)/shard_map/rxiz,rxjz->ij/dot_general | solution.py:28
  311.6 0.6 dynamic-slice
  312.9 101.3 %all-reduce.3.cloned.1.call-done = f32[42,672]{1,0:T(8,128)} async-done(((f32[42,672]{1,0:T(8,128)}), f32[42,672]{1,0:T(8,128)}) %all-reduce.3.cloned.1.call-update) | async-done | bytes 112912
  414.2 1.5 dynamic-slice_multiply_fusion
  (50 shorter events, 2.6 us)
Async XLA Ops:
  7.2 0.7 copy-start
  7.2 133.6 %copy-start.1 = (f32[33,4,42,128]{3,1,2,0:T(4,128)S(1)}, f32[33,4,42,128]{3,1,2,0:T(4,128)}, u32[]{:S(2)}) copy-start(f32[33,4,42,128]{3,1,2,0:T(4,128)} %param.5) | copy-start | bytes 8515588
  7.2 275.2 %all-gather.2.cloned.1.call-start = ((), (), s32[]{:S(2)}) async-start(), calls=%async_computation | async-start | bytes 23396352 | tf_op jit(solution)/shard_map/all_gather | solution.py:42
  140.7 3.4 copy-start.2
  144.2 167.4 %copy-start.3 = (u32[256]{0:T(256)S(1)}, u32[256]{0:T(256)}, u32[]{:S(2)}) copy-start(u32[256]{0:T(256)} %constant.40) | copy-start | bytes 3076
  144.2 270.0 %all-reduce.3.cloned.1.call-start = ((), (), s32[]{:S(2)}) async-start(), calls=%async_computation.1 | async-start | bytes 294912
Sparse Core Ops, SparseCore 0:
  144.3 138.0 all-gather.1
  311.7 102.3 all-reduce.2
where the time goes:
time: 423 us; the launch traced here: 422 us
  waiting for transfers between devices  239 us (57%)
  blocking collectives  81.5 us (19%)
  matrix products  42.7 us (10%)
  other arithmetic  41.8 us (10%)
  between operations  14.9 us (4%)
    all_gather x1, waiting for transfers between devices, on_device(): part_block = line_gram(core, lax.all_gather(core, 'gy', axis=2, tiled=True))  138 us
    unnamed x3, waiting for transfers between devices  101 us
    psum x1, blocking collectives, on_device(): lax.psum(partial_gram, ('gx', 'gy', 'sa')) / (total_x * total_y * total_z)  81.5 us
    dot_general x1, matrix products, line_gram(): return jnp.einsum('rxiz,rxjz->ij', left, right, precision=HIGH)  29.2 us
    another operation x30, other arithmetic, orth(): lower = jnp.linalg.cholesky(inner)  21.5 us
    another operation x20, other arithmetic, orth(): return jax.scipy.linalg.solve_triangular(lower, block.T, lower=True).T  18.8 us
  transfers between devices with their start and end apart: 2, of which 2 were waited for; matrix products, arithmetic and copies ran while one was open for 0% of the time, Pallas kernels for 0%

commit v1 on v0

--- a/solution.py
+++ b/solution.py
@@ -2,6 +2,7 @@
 import jax.numpy as jnp
 from jax import lax
 from jax.sharding import PartitionSpec as P
+from jax.lax import psum
 
 ITERS = 4
 HIGH = lax.Precision.HIGHEST
@@ -36,7 +37,9 @@
     total_z = cells_z * lax.axis_size("sa")
     flat = field.reshape(species, -1)
     partial_gram = jnp.dot(flat, flat.T, precision=HIGH, preferred_element_type=jnp.float32)
-    species_gram = lax.psum(partial_gram, ("gx", "gy", "sa")) / (total_x * total_y * total_z)
+    species_gram = psum(psum(partial_gram, axis_name=("gy", "sa")), axis_name="gx") / (
+        total_x * total_y * total_z
+    )
     basis = leading(species_gram, start, ITERS)
     core = project(basis, field)
     part_block = line_gram(core, lax.all_gather(core, "gy", axis=2, tiled=True))

time: 423 us -> 501 us (1.18)
  blocking collectives: 81.5 us -> 150 us
  waiting for transfers between devices: 239 us -> 249 us
    psum x1 -> x2, blocking collectives: 81.5 us -> 150 us  [the longest x1 124 us: on_device(): psum(partial_gram, axis_name=('gy', 'sa'))]
    all_gather x1, waiting for transfers between devices: 138 us -> 147 us  [on_device(): part_block = line_gram(core, lax.all_gather(core, 'gy', axis=2, tiled=True))]
where the time goes in v1:
time: 501 us
  waiting for transfers between devices  249 us (50%)
  blocking collectives  150 us (30%)
  matrix products  42.7 us (9%)
  other arithmetic  41.8 us (8%)
  between operations  14.9 us (3%)
    all_gather x1, waiting for transfers between devices, on_device(): part_block = line_gram(core, lax.all_gather(core, 'gy', axis=2, tiled=True))  147 us
    psum x1, blocking collectives, on_device(): psum(partial_gram, axis_name=('gy', 'sa'))  124 us
    unnamed x3, waiting for transfers between devices  101 us
    dot_general x1, matrix products, line_gram(): return jnp.einsum('rxiz,rxjz->ij', left, right, precision=HIGH)  29.2 us
    psum x1, blocking collectives, on_device(): psum(psum(partial_gram, axis_name=('gy', 'sa')), axis_name='gx')  26 us
    another operation x30, other arithmetic, orth(): lower = jnp.linalg.cholesky(inner)  21.5 us
    another operation x20, other arithmetic, orth(): return jax.scipy.linalg.solve_triangular(lower, block.T, lower=True).T  18.8 us
  transfers between devices with their start and end apart: 2, of which 2 were waited for; matrix products, arithmetic and copies ran while one was open for 0% of the time, Pallas kernels for 0%

profile of v1, /device:TPU:1, one launch (start us, length us, event | category | flops | bytes accessed | tf_op | source)
XLA Modules:
  0.0 500.7 jit_solution(18278713739232230433)
XLA Ops:
  7.2 0.6 copy-done
  8.1 1.5 cholesky.164
  9.6 0.6 compare_reduce_fusion.9
  10.2 0.6 fusion.27
  10.9 1.2 custom-call.14
  12.1 0.2 fusion.69
  12.5 1.5 cholesky.175
  14.0 0.6 compare_reduce_fusion.8
  14.7 0.6 fusion.28
  15.3 1.2 custom-call.15
  16.6 0.2 fusion.66
  16.8 6.2 %fusion.12 = f32[33,33]{1,0:T(8,128)S(1)} fusion(f32[33,4,42,128]{3,1,2,0:T(4,128)} %param.5), kind=kOutput, calls=%fused_computation.8 | convolution fusion | flops 281014272 | bytes 2842884 | tf_op jit(solution)/shard_map/dot_general | solution.py:39
  22.9 124.2 %psum.14 = f32[33,33]{1,0:T(8,128)S(1)} all-reduce(f32[33,33]{1,0:T(8,128)S(1)} %fusion.12), channel_id=1, replica_groups=mesh['gx'=8,'gy'=16,'sa'=2] {'gy','sa'}, use_global_device_ids=true, to_apply=%region_0.0 | all-reduce | flops 1089 | bytes 8712 | tf_op jit(solution)/shard_map/psum | solution.py:40
  147.2 26.0 %psum.15 = f32[33,33]{1,0:T(8,128)S(1)} all-reduce(f32[33,33]{1,0:T(8,128)S(1)} %psum.14), channel_id=1, replica_groups=mesh['gx'=8,'gy'=16,'sa'=2] {'gx'}, use_global_device_ids=true, to_apply=%region_1.0 | all-reduce | flops 1089 | bytes 8712 | tf_op jit(solution)/shard_map/psum | solution.py:40
  173.6 1.5 cholesky.186
  175.1 0.6 compare_reduce_fusion.7
  175.7 0.6 fusion.29
  176.4 1.2 custom-call.16
  177.6 0.2 fusion.62
  178.0 1.5 cholesky.197
  179.5 0.6 compare_reduce_fusion.6
  180.2 0.6 fusion.30
  180.8 1.2 custom-call.17
  182.1 0.2 fusion.59
  182.3 0.2 fusion.19
  182.6 1.5 cholesky.208
  184.2 0.6 compare_reduce_fusion.5
  184.8 0.6 fusion.31
  185.5 1.2 custom-call.18
  186.7 0.2 fusion.55
  187.1 1.5 cholesky.219
  188.6 0.6 compare_reduce_fusion.4
  189.3 0.6 fusion.32
  189.9 1.2 custom-call.19
  191.1 0.2 fusion.52
  191.3 0.2 fusion.17
  191.7 1.5 cholesky.230
  193.2 0.6 compare_reduce_fusion.3
  193.9 0.6 fusion.33
  194.5 1.2 custom-call.20
  195.8 0.2 fusion.48
  196.2 1.5 cholesky.241
  197.7 0.6 compare_reduce_fusion.2
  198.3 0.6 fusion.34
  199.0 1.2 custom-call.21
  200.2 0.2 fusion.45
  200.4 0.2 fusion.15
  200.8 1.5 cholesky.252
  202.3 0.6 compare_reduce_fusion.1
  202.9 0.6 fusion.35
  203.6 1.2 custom-call.22
  204.8 0.2 fusion.41
  205.3 1.5 cholesky.263
  206.8 0.6 compare_reduce_fusion
  207.4 0.6 fusion.36
  208.1 1.2 custom-call.23
  209.3 0.2 fusion.38
  209.5 3.4 fusion.2
  212.9 0.2 all-reduce.3.cloned.1.call-start
  213.2 147.5 %all-gather.2.cloned.1.call-done = f32[16,4,672,128]{3,0,2,1:T(8,128)} async-done(((f32[16,4,42,128]{3,0,2,1:T(8,128)}), f32[16,4,672,128]{3,0,2,1:T(8,128)}) %all-gather.2.cloned.1.call-update) | async-done | bytes 22020112 | tf_op jit(solution)/shard_map/all_gather | solution.py:45
  360.6 29.2 %fusion.7 = f32[42,672]{1,0:T(8,128)} fusion(f32[16,4,672,128]{3,0,2,1:T(8,128)} %all-gather.2.cloned.1.call-done, f32[16,4,42,128]{3,0,2,1:T(8,128)} %fusion.2), kind=kOutput, calls=%fused_computation.7 | convolution fusion | flops 2774532096 | bytes 23509248 | tf_op jit(solution)/shard_map/rxiz,rxjz->ij/dot_general | solution.py:29
  389.9 0.6 dynamic-slice
  391.1 101.3 %all-reduce.3.cloned.1.call-done = f32[42,672]{1,0:T(8,128)} async-done(((f32[42,672]{1,0:T(8,128)}), f32[42,672]{1,0:T(8,128)}) %all-reduce.3.cloned.1.call-update) | async-done | bytes 112912
  492.4 1.5 dynamic-slice_multiply_fusion
  (51 shorter events, 2.7 us)
Async XLA Ops:
  7.2 0.7 copy-start
  7.2 202.3 %copy-start.1 = (f32[33,4,42,128]{3,1,2,0:T(4,128)S(1)}, f32[33,4,42,128]{3,1,2,0:T(4,128)}, u32[]{:S(2)}) copy-start(f32[33,4,42,128]{3,1,2,0:T(4,128)} %param.5) | copy-start | bytes 8515588
  7.2 353.5 %all-gather.2.cloned.1.call-start = ((), (), s32[]{:S(2)}) async-start(), calls=%async_computation | async-start | bytes 23396352 | tf_op jit(solution)/shard_map/all_gather | solution.py:45
  209.5 3.4 copy-start.2
  212.9 176.9 %copy-start.3 = (u32[256]{0:T(256)S(1)}, u32[256]{0:T(256)}, u32[]{:S(2)}) copy-start(u32[256]{0:T(256)} %constant.40) | copy-start | bytes 3076
  212.9 279.5 %all-reduce.3.cloned.1.call-start = ((), (), s32[]{:S(2)}) async-start(), calls=%async_computation.1 | async-start | bytes 294912
Sparse Core Ops, SparseCore 0:
  213.0 147.5 all-gather.1
  390.0 102.3 all-reduce.2
